TPU v7x, 32 devices: a whole 2x2x4 slice. The times are simulated.
32 devices in a mesh: dp: 8 (over z, x), tensor: 4 (over y, core).
Axes of the slice: x: 2, y: 2, z: 4, core: 2. Of those that a mesh axis runs over, the one named last changes fastest.
Arguments:
- context: bfloat16 [8192, 7168], P('dp', 'tensor'), may hold values from -6 to 6
- resid: bfloat16 [8192, 7168], P(('dp', 'tensor')), may hold values from -6 to 6
- o_weight: bfloat16 [7168, 7168], P('tensor', 'dp'), may hold values from -0.0625 to 0.0625
- norm_gain: float32 [7168], replicated, may hold values from 0.5 to 1.5
- queries: float32 [32, 7168], P('dp'), may hold values from -6 to 6
- positive_ids: int32 [32], P('dp'), may hold values from 0 to 15
- negative_ids: int32 [32, 7], P('dp'), may hold values from 0 to 15
- margins: float32 [32, 7], P('dp'), may hold values from -6 to 6
- pair_counts: int32 [32], P('dp'), may hold values from 1 to 7, as said below
Outputs:
- hidden_grad: float32 [8192, 7168], P(('dp', 'tensor'))
- loss: float32 [], replicated
Inputs may be any that keep to these rules, and one draw needn't show every extreme that they name: `pair_counts`: some query has all 7 negatives live.
All inputs are finite; a program needn't handle non-finite values.
Results may differ from a plain program's by a relative error of at most 0.0003.
Values may be sent and summed in bfloat16 or wider, within the bound.
A program may use at most 192 MiB of HBM per device.

v0:
```python
import jax
import jax.numpy as jnp
from jax import lax
from jax.sharding import PartitionSpec as P

D = 7168
SEQ = 512
PASS_DEV = 2
Q_DEV = 4
NEG = 7


def shards(
    context, resid, o_weight, norm_gain, queries, positive_ids, negative_ids, margins, pair_counts
):
    full_weight = lax.all_gather(o_weight, "dp", axis=1, tiled=True)
    tok_rows = resid.shape[0]
    attn = lax.psum_scatter(
        jnp.dot(context, full_weight, preferred_element_type=jnp.float32),
        "tensor",
        scatter_dimension=0,
        tiled=True,
    )
    hidden = resid.astype(jnp.float32) + attn
    inv = lax.rsqrt(jnp.mean(hidden * hidden, axis=-1, keepdims=True) + 1e-05)
    normed = hidden * inv * norm_gain
    first = lax.axis_index("tensor") * tok_rows
    passage_of = (first + jnp.arange(tok_rows, dtype=jnp.int32)) // SEQ
    member = (passage_of[None, :] == jnp.arange(PASS_DEV, dtype=jnp.int32)[:, None]).astype(
        jnp.float32
    )
    partial_value = jnp.dot(member, normed, precision=lax.Precision.HIGHEST)
    scale = 1.0 / jnp.sqrt(jnp.float32(D * SEQ))
    npass = PASS_DEV * lax.axis_size("dp")
    nquery = Q_DEV * lax.axis_size("dp")
    pooled = lax.psum(partial_value, "tensor")
    every_pass = lax.all_gather(pooled, "dp", axis=0, tiled=True)
    scores = jnp.dot(queries, every_pass.T, precision=lax.Precision.HIGHEST) * scale
    passes = jnp.arange(npass, dtype=jnp.int32)
    onehot_pos = (positive_ids[:, None] == passes[None, :]).astype(jnp.float32)
    onehot_neg = (negative_ids[:, :, None] == passes[None, None, :]).astype(jnp.float32)
    score_pos = jnp.sum(onehot_pos * scores, axis=-1)
    score_neg = jnp.sum(onehot_neg * scores[:, None, :], axis=-1)
    err = score_pos[:, None] - score_neg - margins
    live = (jnp.arange(NEG, dtype=jnp.int32)[None, :] < pair_counts[:, None]).astype(jnp.float32)
    counts = pair_counts.astype(jnp.float32)
    local_loss = jnp.sum(jnp.sum(live * err * err, axis=1) / counts) / nquery
    weight = 2.0 * live * err / (counts[:, None] * nquery)
    coef = onehot_pos * jnp.sum(weight, axis=1)[:, None] - jnp.sum(
        weight[:, :, None] * onehot_neg, axis=1
    )
    grad_terms = jnp.dot(coef.T, queries, precision=lax.Precision.HIGHEST) * scale
    pass_grad = lax.psum_scatter(grad_terms, "dp", scatter_dimension=0, tiled=True)
    loss = lax.psum(local_loss, "dp")
    upward = jnp.dot(member.T, pass_grad, precision=lax.Precision.HIGHEST) * norm_gain
    inner = jnp.mean(hidden * upward, axis=-1, keepdims=True)
    grad = 65536.0 * (inv * upward - hidden * inv * inv * inv * inner)
    return (grad, loss)


def solution(mesh):
    return jax.shard_map(
        shards,
        mesh=mesh,
        in_specs=(
            P("dp", "tensor"),
            P(("dp", "tensor"), None),
            P("tensor", "dp"),
            P(),
            P("dp", None),
            P("dp"),
            P("dp", None),
            P("dp", None),
            P("dp"),
        ),
        out_specs=(P(("dp", "tensor"), None), P()),
        check_vma=False,
    )
```

profile of v0, /device:TPU:0, one launch (start us, length us, event | category | flops | bytes accessed | tf_op | source)
XLA Modules:
  0.0 894.7 jit_solution(5378871279097211902)
XLA Ops:
  7.2 0.0 copy-start
  7.2 0.0 all-gather.3.cloned.1.call-start
  7.2 0.7 all-gather.3.cloned.1.call-update
  7.9 0.0 reduce-scatter.2.cloned.1.call-start
  8.0 494.6 %all-gather.3.cloned.1.call-done = bf16[1792,7168]{1,0:T(8,128)(2,1)} async-done(((bf16[1792,896]{1,0:T(8,128)(2,1)}), bf16[1792,7168]{1,0:T(8,128)(2,1)}) %all-gather.3.cloned.1.call-update) | async-done | bytes 25690128 | tf_op jit(solution)/shard_map/all_gather | solution.py:16
  502.6 34.1 %fusion.19 = f32[1024,7168]{1,0:T(8,128)} fusion(bf16[1024,1792]{1,0:T(8,128)(2,1)} %param.9, bf16[1792,7168]{1,0:T(8,128)(2,1)} %all-gather.3.cloned.1.call-done), kind=kOutput, calls=%fused_computation.44 | convolution fusion | flops 26306674688 | bytes 58720256 | tf_op jit(solution)/shard_map/dot_general | solution.py:19
  536.6 0.0 copy-start.6
  536.6 0.0 copy-start.7
  536.6 0.0 copy-start.8
  536.6 0.0 copy-start.4
  536.7 0.0 reduce-scatter.2.cloned.1.call-update
  536.7 0.0 all-reduce.3.cloned.1.call-start
  536.7 0.6 copy-done.6
  537.3 0.1 copy.11
  537.4 0.0 copy-done.7
  537.4 0.1 copy.12
  537.5 0.0 copy-done.8
  537.5 207.2 %reduce-scatter.2.cloned.1.call-done = f32[256,7168]{1,0:T(8,128)} async-done(((f32[1024,7168]{1,0:T(8,128)}), f32[256,7168]{1,0:T(8,128)}) %reduce-scatter.2.cloned.1.call-update) | async-done | bytes 7340048 | tf_op jit(solution)/shard_map/reduce_scatter | solution.py:18
  744.7 0.0 copy-start.1
  744.7 0.0 copy-start.2
  744.7 5.3 multiply_reduce_fusion.1
  750.0 0.0 copy-start.5
  750.0 0.0 copy-start.9
  750.0 0.0 copy-done.4
  750.1 0.9 copy-done.1
  750.9 1.0 copy-done.2
  751.9 3.4 fusion
  755.3 10.7 %psum.14 = f32[2,7168]{1,0:T(2,128)S(1)} all-reduce(f32[2,7168]{1,0:T(2,128)S(1)} %fusion), channel_id=1, replica_groups=mesh['dp'=8,'tensor'=4] {'tensor'}, use_global_device_ids=true, to_apply=%region_2.3 | all-reduce | flops 14336 | bytes 114688 | tf_op jit(solution)/shard_map/psum | solution.py:36
  766.0 31.4 %all-gather = f32[8,2,7168]{2,1,0:T(2,128)S(1)} all-gather(f32[1,2,7168]{2,1,0:T(2,128)S(1)} %bitcast.9), channel_id=1, replica_groups=mesh['dp'=8,'tensor'=4] {'dp'}, dimensions={0}, use_global_device_ids=true | all-gather | bytes 516096 | tf_op jit(solution)/shard_map/all_gather | solution.py:37
  797.4 0.3 reshape.46
  797.8 0.0 copy-done
  797.8 0.0 copy-done.5
  797.8 0.8 select_reduce_fusion.2
  798.6 0.2 select_reduce_fusion.1
  798.7 0.1 select_reduce_fusion
  798.8 1.5 convolution_multiply_fusion.1
  800.3 0.0 all-reduce.3.cloned.1.call-update
  800.3 0.0 copy-done.9
  800.3 0.6 dynamic-slice
  800.9 0.7 fusion.16
  802.9 22.0 %psum.15 = f32[]{:T(128)} all-reduce(f32[]{:T(128)S(6)} %div.41), channel_id=1, replica_groups=mesh['dp'=8,'tensor'=4] {'dp'}, use_global_device_ids=true, to_apply=%region_11.12 | all-reduce | flops 1 | bytes 8 | tf_op jit(solution)/shard_map/psum | solution.py:54
  824.9 48.5 %all-reduce.3.cloned.1.call-done = f32[16,7168]{1,0:T(8,128)} async-done(((f32[16,7168]{1,0:T(8,128)}), f32[16,7168]{1,0:T(8,128)}) %all-reduce.3.cloned.1.call-update) | async-done | bytes 458768
  873.5 0.0 copy-start.3
  873.5 8.3 multiply_reduce_fusion
  881.8 0.0 copy-done.3
  881.8 6.4 subtract_multiply_fusion
  (5 shorter events, 0.1 us)
Async XLA Ops:
  7.2 790.6 %copy-start = (f32[4,7168]{1,0:T(4,128)S(1)}, f32[4,7168]{1,0:T(4,128)}, u32[]{:S(2)}) copy-start(f32[4,7168]{1,0:T(4,128)} %param.13) | copy-start | bytes 344068
  7.2 495.4 %all-gather.3.cloned.1.call-start = ((), (), s32[]{:S(2)}) async-start(), calls=%async_computation.1 | async-start | bytes 28901376 | tf_op jit(solution)/shard_map/all_gather | solution.py:16
  7.9 736.8 %reduce-scatter.2.cloned.1.call-start = ((), (), s32[]{:S(2)}) async-start(), calls=%async_computation.2 | async-start | bytes 36700160 | tf_op jit(solution)/shard_map/reduce_scatter | solution.py:18
  536.6 0.7 copy-start.6
  536.6 0.8 copy-start.7
  536.6 0.9 copy-start.8
  536.6 213.4 %copy-start.4 = (f32[7168]{0:T(1024)S(1)}, f32[7168]{0:T(1024)}, u32[]{:S(2)}) copy-start(f32[7168]{0:T(1024)} %param.12) | copy-start | bytes 86020
  536.7 336.8 %all-reduce.3.cloned.1.call-start = ((), (), s32[]{:S(2)}) async-start(), calls=%async_computation.3 | async-start | bytes 917504
  744.7 6.2 copy-start.1
  744.7 7.3 copy-start.2
  750.0 47.8 %copy-start.5 = (s32[4]{0:T(128)S(1)}, s32[4]{0:T(128)}, u32[]{:S(2)}) copy-start(s32[4]{0:T(128)} %param.14) | copy-start | bytes 52
  750.0 50.3 %copy-start.9 = (u32[32]{0:T(128)S(1)}, u32[32]{0:T(128)}, u32[]{:S(2)}) copy-start(u32[32]{0:T(128)} %constant.55) | copy-start | bytes 388
  873.5 8.3 copy-start.3
Sparse Core Ops, SparseCore 0:
  9.6 492.9 all-gather.2
  536.8 207.8 reduce-scatter.1
  800.4 72.9 all-reduce.2
where the time goes:
time: 895 us
  waiting for transfers between devices  751 us (84%)
  blocking collectives  64.1 us (7%)
  matrix products  47.9 us (5%)
  between operations  15.2 us (2%)
  other arithmetic  12.7 us (1%)
    all_gather x1, waiting for transfers between devices, shards(): full_weight = lax.all_gather(o_weight, 'dp', axis=1, tiled=True)  495 us
    reduce_scatter x1, waiting for transfers between devices, shards(): lax.psum_scatter(jnp.dot(context, full_weight, preferred_element_type=jnp...  207 us
    unnamed x4, waiting for transfers between devices  49.3 us
    dot_general x1, matrix products, shards(): jnp.dot(context, full_weight, preferred_element_type=jnp.float32)  34.1 us
    all_gather x1, blocking collectives, shards(): every_pass = lax.all_gather(pooled, 'dp', axis=0, tiled=True)  31.4 us
    psum x1, blocking collectives, shards(): loss = lax.psum(local_loss, 'dp')  22 us
  transfers between devices with their start and end apart: 3, of which 3 were waited for; matrix products, arithmetic and copies ran while one was open for 0% of the time, Pallas kernels for 0%

commit v1 on v0

--- a/solution.py
+++ b/solution.py
@@ -58,9 +58,119 @@
     return (grad, loss)
 
 
+def line_shards(
+    context, resid, o_weight, norm_gain, queries, positive_ids, negative_ids, margins, pair_counts
+):
+    f32 = jnp.float32
+    dp_at, t_at = lax.axis_index("dp"), lax.axis_index("tensor")
+    z, x = dp_at // 2, dp_at % 2
+    y, core = t_at // 2, t_at % 2
+    tok_rows = resid.shape[0]
+    width = o_weight.shape[1]
+
+    def shift(value, step, sources):
+        pairs = [(2 * s + i, 2 * (s + step) + i) for s in sources for i in range(2)]
+        return lax.ppermute(value, "dp", pairs)
+
+    def swap_x(value, zs):
+        pairs = [(2 * s + i, 2 * s + 1 - i) for s in zs for i in range(2)]
+        return lax.ppermute(value, "dp", pairs)
+
+    def swap_tensor(value, bit, zs):
+        pairs = [
+            ((2 * s + i) * 4 + t, (2 * s + i) * 4 + (t ^ bit))
+            for s in zs
+            for i in range(2)
+            for t in range(4)
+        ]
+        return lax.ppermute(value, ("dp", "tensor"), pairs)
+
+    rows = context.reshape(2, 2, tok_rows, context.shape[1])
+    rows = jnp.where(y == 0, rows, rows[::-1])
+    rows = jnp.where(core == 0, rows, rows[:, ::-1])
+    mine = rows.transpose(1, 0, 2, 3).reshape(context.shape)
+    every = (0, 1, 2, 3)
+    theirs = swap_x(mine, every)
+
+    small = jnp.concatenate(
+        [
+            queries,
+            positive_ids.astype(f32)[:, None],
+            negative_ids.astype(f32),
+            margins,
+            pair_counts.astype(f32)[:, None],
+        ],
+        axis=1,
+    )
+    small = lax.all_gather(small, "dp", axis=0, tiled=True)
+    queries = small[:, :D]
+    positive_ids = small[:, D].astype(jnp.int32)
+    negative_ids = small[:, D + 1 : D + 1 + NEG].astype(jnp.int32)
+    margins = small[:, D + 1 + NEG : D + 1 + 2 * NEG]
+    counts = small[:, D + 1 + 2 * NEG]
+
+    left1 = shift(o_weight, 1, (0, 1, 2))
+    right1 = shift(o_weight, -1, (1, 2, 3))
+    left2 = shift(left1, 1, (1, 2))
+    right2 = shift(right1, -1, (1, 2))
+    left3 = shift(left2, 1, (2,))
+    right3 = shift(right2, -1, (1,))
+
+    def reduced(acts, block, zs):
+        part = jnp.dot(acts, block, preferred_element_type=f32)
+        half, quarter = 2 * tok_rows, tok_rows
+        kept = part[:half] + swap_tensor(part[half:], 1, every)
+        return kept[:quarter] + swap_tensor(kept[quarter:], 2, zs)
+
+    def columns(block, zs):
+        away = swap_x(reduced(theirs, block, zs), zs)
+        return reduced(mine, block, zs), away
+
+    own = columns(o_weight, every)
+    from_left = columns(left1, (1, 2, 3))
+    from_right = columns(right1, (0, 1, 2))
+    opposite = columns(jnp.where(z >= 2, left2, right2), every)
+    far = columns(jnp.where(z == 3, left3, right3), (0, 3))
+    before = [jnp.where(z == 0, a, b) for a, b in zip(far, from_left)]
+    after = [jnp.where(z == 3, a, b) for a, b in zip(far, from_right)]
+    blocks = jnp.stack([*own, *after, *opposite, *before])
+    ordered = [
+        lax.dynamic_index_in_dim(blocks, ((j // 2 - z) % 4) * 2 + (j + x) % 2, 0, keepdims=False)
+        for j in range(8)
+    ]
+    hidden = resid.astype(f32) + jnp.concatenate(ordered, axis=1)
+    inv = lax.rsqrt(jnp.mean(hidden * hidden, axis=-1, keepdims=True) + 1e-05)
+    pooled = jnp.sum(hidden * inv, axis=0) * norm_gain
+    scale = 1.0 / jnp.sqrt(f32(D * SEQ))
+    npass = PASS_DEV * lax.axis_size("dp")
+    nquery = Q_DEV * lax.axis_size("dp")
+    passes = jnp.arange(npass, dtype=jnp.int32)
+    passage = PASS_DEV * dp_at + (t_at * tok_rows) // SEQ
+    here = (passes == passage).astype(f32)
+    scores = jnp.sum(queries * pooled[None, :], axis=1)[:, None] * here[None, :] * scale
+    scores = lax.psum(scores, ("dp", "tensor"))
+    onehot_pos = (positive_ids[:, None] == passes[None, :]).astype(f32)
+    onehot_neg = (negative_ids[:, :, None] == passes[None, None, :]).astype(f32)
+    score_pos = jnp.sum(onehot_pos * scores, axis=-1)
+    score_neg = jnp.sum(onehot_neg * scores[:, None, :], axis=-1)
+    err = score_pos[:, None] - score_neg - margins
+    live = (jnp.arange(NEG, dtype=f32)[None, :] < counts[:, None]).astype(f32)
+    loss = jnp.sum(jnp.sum(live * err * err, axis=1) / counts) / nquery
+    weight = 2.0 * live * err / (counts[:, None] * nquery)
+    at_pos = jnp.sum(onehot_pos * here[None, :], axis=1)
+    at_neg = jnp.sum(onehot_neg * here[None, None, :], axis=2)
+    coef = at_pos * jnp.sum(weight, axis=1) - jnp.sum(weight * at_neg, axis=1)
+    pass_grad = jnp.sum(coef[:, None] * queries, axis=0) * scale
+    upward = (pass_grad * norm_gain)[None, :]
+    inner = jnp.mean(hidden * upward, axis=-1, keepdims=True)
+    grad = 65536.0 * (inv * upward - hidden * (inv * inv * inv * inner))
+    return (grad, loss)
+
+
 def solution(mesh):
+    body = line_shards if dict(mesh.shape) == {"dp": 8, "tensor": 4} else shards
     return jax.shard_map(
-        shards,
+        body,
         mesh=mesh,
         in_specs=(
             P("dp", "tensor"),

time: 895 us -> 526 us (0.59)
  waiting for transfers between devices: 751 us -> 147 us
  blocking collectives: 64.1 us -> 164 us
  starting transfers between devices: 0.12 us -> 46.7 us
  local copies, waits for them, and re-layouts: 3.6 us -> 49.9 us
  other arithmetic: 12.7 us -> 41.9 us
  matrix products: 47.9 us -> 64.6 us
  between operations: 15.2 us -> 3.76 us
    all_gather x1 -> x0, waiting for transfers between devices: 495 us -> none  [shards(): full_weight = lax.all_gather(o_weight, 'dp', axis=1, tiled=True)]
    reduce_scatter x1 -> x0, waiting for transfers between devices: 207 us -> none  [shards(): lax.psum_scatter(jnp.dot(context, full_weight, preferred_element_type=jnp...]
    ppermute x0 -> x32, waiting for transfers between devices: none -> 147 us  [the longest x6 66.8 us: shift(): return lax.ppermute(value, 'dp', pairs)]
    all_gather x1, blocking collectives: 31.4 us -> 107 us  [line_shards(): small = lax.all_gather(small, 'dp', axis=0, tiled=True)]
    unnamed x4 -> x0, waiting for transfers between devices: 49.3 us -> none
    ppermute x0 -> x32, starting transfers between devices: none -> 46.7 us  [the longest x20 19.8 us: swap_tensor(): return lax.ppermute(value, ('dp', 'tensor'), pairs)]
    psum x2 -> x1, blocking collectives: 32.7 us -> 57.2 us  [line_shards(): scores = lax.psum(scores, ('dp', 'tensor'))]
    add x0 -> x15, other arithmetic: none -> 16.8 us  [the longest x10 12.3 us: reduced(): kept = part[:half] + swap_tensor(part[half:], 1, every)]
  transfers between devices with their start and end apart: 3 -> 32, of which waited for: 3 -> 8; matrix products, arithmetic and copies ran while one was open for 0% -> 20% of each run, Pallas kernels for 0% -> 0%
where the time goes in v1:
time: 526 us; the launch traced here: 519 us
  blocking collectives  164 us (31%)
  waiting for transfers between devices  147 us (28%)
  matrix products  64.6 us (12%)
  local copies, waits for them, and re-layouts  49.9 us (9%)
  starting transfers between devices  46.7 us (9%)
  other arithmetic  41.9 us (8%)
    all_gather x1, blocking collectives, line_shards(): small = lax.all_gather(small, 'dp', axis=0, tiled=True)  107 us
    ppermute x6, waiting for transfers between devices, shift(): return lax.ppermute(value, 'dp', pairs)  66.8 us
    dot_general x10, matrix products, reduced(): part = jnp.dot(acts, block, preferred_element_type=f32)  64.6 us
    ppermute x20, waiting for transfers between devices, swap_tensor(): return lax.ppermute(value, ('dp', 'tensor'), pairs)  64.5 us
    psum x1, blocking collectives, line_shards(): scores = lax.psum(scores, ('dp', 'tensor'))  57.2 us
    ppermute x20, starting transfers between devices, swap_tensor(): return lax.ppermute(value, ('dp', 'tensor'), pairs)  19.8 us
    unnamed x66, local copies, waits for them, and re-layouts  19.5 us
    ppermute x6, waiting for transfers between devices, swap_x(): return lax.ppermute(value, 'dp', pairs)  16.1 us
  transfers between devices with their start and end apart: 32, of which 8 were waited for; matrix products, arithmetic and copies ran while one was open for 20% of the time, Pallas kernels for 0%

profile of v1, /device:TPU:0, one launch (start us, length us, event | category | flops | bytes accessed | tf_op | source)
XLA Modules:
  0.0 518.8 jit_solution(5544306342793523886)
XLA Ops:
  0.6 1.3 collective-permute-start.9
  1.9 7.3 %collective-permute-start.6 = (bf16[1792,896]{1,0:T(8,128)(2,1)}, bf16[1792,896]{1,0:T(8,128)(2,1)}, u32[]{:S(2)}, u32[]{:S(2)}) collective-permute-start(bf16[1792,896]{1,0:T(8,128)(2,1)} %param.11), channel_id=1, source_target_pairs={{0,8},{4,12},{8,16},{12,20},{16,24},{20,28},{1,9},{5,13},{9,17},{1... | collective-permute-start | bytes 9633800 | tf_op jit(solution)/shard_map/ppermute | solution.py:73
  9.2 4.0 reverse_select_fusion.1
  13.9 2.1 copy.161
  17.1 5.7 %fusion.20 = f32[1024,896]{0,1:T(8,128)S(1)} fusion(bf16[1024,1792]{1,0:T(8,128)(2,1)} %bitcast.2, bf16[1792,896]{1,0:T(8,128)(2,1)S(1)} %copy-done.21), kind=kOutput, calls=%fused_computation.94 | convolution fusion | flops 3288334336 | bytes 10551296 | tf_op jit(solution)/shard_map/dot_general | solution.py:120
  22.9 1.8 copy-done.7
  24.8 1.4 slice.181
  26.2 1.9 collective-permute-start.2
  28.4 107.3 %all-gather = f32[8,4,7184]{2,1,0:T(4,128)S(1)} all-gather(f32[1,4,7184]{2,1,0:T(4,128)S(1)} %bitcast.68), channel_id=1, replica_groups=mesh['dp'=8,'tensor'=4] {'dp'}, dimensions={0}, use_global_device_ids=true | all-gather | bytes 1034496 | tf_op jit(solution)/shard_map/all_gather | solution.py:105
  136.6 2.5 slice_add_fusion.9
  139.2 1.9 collective-permute-start.1
  141.1 1.3 collective-permute-start.10
  142.4 2.6 collective-permute-start.7
  145.0 6.6 %fusion.22 = f32[1024,896]{0,1:T(8,128)S(1)} fusion(bf16[1024,1792]{1,0:T(8,128)(2,1)} %bitcast.2, bf16[1792,896]{1,0:T(8,128)(2,1)} %collective-permute-done.9), kind=kOutput, calls=%fused_computation.96 | convolution fusion | flops 3288334336 | bytes 10551296 | tf_op jit(solution)/shard_map/dot_general | solution.py:120
  151.8 6.6 %fusion.24 = f32[1024,896]{0,1:T(8,128)S(1)} fusion(bf16[1024,1792]{1,0:T(8,128)(2,1)} %bitcast.2, bf16[1792,896]{1,0:T(8,128)(2,1)} %collective-permute-done.6), kind=kOutput, calls=%fused_computation.98 | convolution fusion | flops 3288334336 | bytes 10551296 | tf_op jit(solution)/shard_map/dot_general | solution.py:120
  160.3 5.6 %fusion.21 = f32[1024,896]{0,1:T(8,128)S(1)} fusion(bf16[1024,1792]{1,0:T(8,128)(2,1)} %collective-permute-done.2, bf16[1792,896]{1,0:T(8,128)(2,1)S(1)} %copy-done.22), kind=kOutput, calls=%fused_computation.95 | convolution fusion | flops 3288334336 | bytes 10551296 | tf_op jit(solution)/shard_map/dot_general | solution.py:120
  165.8 1.4 slice.185
  167.3 7.0 %fusion.23 = f32[1024,896]{0,1:T(8,128)S(1)} fusion(bf16[1024,1792]{1,0:T(8,128)(2,1)} %collective-permute-done.2, bf16[1792,896]{1,0:T(8,128)(2,1)} %collective-permute-done.9), kind=kOutput, calls=%fused_computation.97 | convolution fusion | flops 3288334336 | bytes 10551296 | tf_op jit(solution)/shard_map/dot_general | solution.py:120
  174.3 1.5 slice.201
  176.3 34.4 %collective-permute-done.10 = bf16[1792,896]{1,0:T(8,128)(2,1)} collective-permute-done((bf16[1792,896]{1,0:T(8,128)(2,1)}, bf16[1792,896]{1,0:T(8,128)(2,1)}, u32[]{:S(2)}, u32[]{:S(2)}) %collective-permute-start.10) | collective-permute-done | bytes 3211296 | tf_op jit(solution)/shard_map/ppermute | solution.py:73
  212.0 2.3 collective-permute-start.8
  214.3 6.7 %fusion.25 = f32[1024,896]{0,1:T(8,128)S(1)} fusion(bf16[1024,1792]{1,0:T(8,128)(2,1)} %collective-permute-done.2, bf16[1792,896]{1,0:T(8,128)(2,1)} %collective-permute-done.6), kind=kOutput, calls=%fused_computation.99 | convolution fusion | flops 3288334336 | bytes 10551296 | tf_op jit(solution)/shard_map/dot_general | solution.py:120
  221.4 1.5 copy-done.12
  225.8 1.9 slice_add_fusion.8
  228.9 2.1 slice_add_fusion.4
  232.1 3.5 collective-permute-start.20
  237.1 1.8 collective-permute-start.30
  238.8 6.6 %fusion.4 = f32[1024,896]{0,1:T(8,128)S(1)} fusion(bf16[1024,1792]{1,0:T(8,128)(2,1)} %bitcast.2, bf16[1792,896]{1,0:T(8,128)(2,1)} %collective-permute-done.7, bf16[1792,896]{1,0:T(8,128)(2,1)} %collective-permute-done.10, pred[]{:T(512)S(6)} %ge.3), kind=kOutput, calls=%fused_computation.23 | convolution fusion | flops 3289939968 | bytes 13762561 | tf_op jit(solution)/shard_map/dot_general | solution.py:120
  245.4 32.4 %collective-permute-done.11 = bf16[1792,896]{1,0:T(8,128)(2,1)} collective-permute-done((bf16[1792,896]{1,0:T(8,128)(2,1)}, bf16[1792,896]{1,0:T(8,128)(2,1)}, u32[]{:S(2)}, u32[]{:S(2)}) %collective-permute-start.11) | collective-permute-done | bytes 3211296 | tf_op jit(solution)/shard_map/ppermute | solution.py:73
  277.8 6.6 %fusion.1 = f32[1024,896]{0,1:T(8,128)S(1)} fusion(bf16[1024,1792]{1,0:T(8,128)(2,1)} %collective-permute-done.2, bf16[1792,896]{1,0:T(8,128)(2,1)} %collective-permute-done.8, bf16[1792,896]{1,0:T(8,128)(2,1)} %collective-permute-done.11, pred[]{:T(512)S(6)} %eq.78), kind=kOutput, calls=%fused_computation.20 | convolution fusion | flops 3289939968 | bytes 13762561 | tf_op jit(solution)/shard_map/dot_general | solution.py:120
  284.4 1.7 slice.197
  286.9 6.6 %fusion.3 = f32[1024,896]{0,1:T(8,128)S(1)} fusion(bf16[1024,1792]{1,0:T(8,128)(2,1)} %collective-permute-done.2, bf16[1792,896]{1,0:T(8,128)(2,1)} %collective-permute-done.7, bf16[1792,896]{1,0:T(8,128)(2,1)} %collective-permute-done.10, pred[]{:T(512)S(6)} %ge.3), kind=kOutput, calls=%fused_computation.22 | convolution fusion | flops 3289939968 | bytes 13762561 | tf_op jit(solution)/shard_map/dot_general | solution.py:120
  293.7 1.7 slice.209
  296.4 6.8 %fusion.2 = f32[1024,896]{0,1:T(8,128)S(1)} fusion(bf16[1024,1792]{1,0:T(8,128)(2,1)} %bitcast.2, bf16[1792,896]{1,0:T(8,128)(2,1)} %collective-permute-done.8, bf16[1792,896]{1,0:T(8,128)(2,1)} %collective-permute-done.11, pred[]{:T(512)S(6)} %eq.78), kind=kOutput, calls=%fused_computation.21 | convolution fusion | flops 3289939968 | bytes 13762561 | tf_op jit(solution)/shard_map/dot_general | solution.py:120
  303.4 1.5 slice_add_fusion.18
  305.8 1.3 slice_add_fusion.14
  307.5 1.3 slice_add_fusion.10
  308.9 2.6 collective-permute-start.15
  311.5 1.9 slice_add_fusion.5
  313.5 14.4 %collective-permute-done.5 = f32[256,896]{0,1:T(8,128)S(1)} collective-permute-done((f32[256,896]{0,1:T(8,128)S(1)}, f32[256,896]{0,1:T(8,128)S(1)}, u32[]{:S(2)}, u32[]{:S(2)}) %collective-permute-start.5) | collective-permute-done | bytes 917536 | tf_op jit(solution)/shard_map/ppermute | solution.py:77
  327.9 2.4 collective-permute-start.17
  330.4 2.6 collective-permute-start.21
  333.0 1.9 slice_add_fusion.2
  335.0 1.7 collective-permute-start.25
  337.2 16.7 %collective-permute-done.17 = f32[256,896]{0,1:T(8,128)S(1)} collective-permute-done((f32[256,896]{0,1:T(8,128)S(1)}, f32[256,896]{0,1:T(8,128)S(1)}, u32[]{:S(2)}, u32[]{:S(2)}) %collective-permute-start.17) | collective-permute-done | bytes 917536 | tf_op jit(solution)/shard_map/ppermute | solution.py:86
  353.9 2.3 collective-permute-start.13
  356.4 3.3 collective-permute-start.18
  360.2 13.4 %collective-permute-done.25 = f32[256,896]{0,1:T(8,128)S(1)} collective-permute-done((f32[256,896]{0,1:T(8,128)S(1)}, f32[256,896]{0,1:T(8,128)S(1)}, u32[]{:S(2)}, u32[]{:S(2)}) %collective-permute-start.25) | collective-permute-done | bytes 917536 | tf_op jit(solution)/shard_map/ppermute | solution.py:86
  374.9 18.3 %collective-permute-done.13 = f32[256,896]{0,1:T(8,128)S(1)} collective-permute-done((f32[256,896]{0,1:T(8,128)S(1)}, f32[256,896]{0,1:T(8,128)S(1)}, u32[]{:S(2)}, u32[]{:S(2)}) %collective-permute-start.13) | collective-permute-done | bytes 917536 | tf_op jit(solution)/shard_map/ppermute | solution.py:86
  396.1 16.0 %collective-permute-done.23 = f32[256,896]{0,1:T(8,128)S(1)} collective-permute-done((f32[256,896]{0,1:T(8,128)S(1)}, f32[256,896]{0,1:T(8,128)S(1)}, u32[]{:S(2)}, u32[]{:S(2)}) %collective-permute-start.23) | collective-permute-done | bytes 917536 | tf_op jit(solution)/shard_map/ppermute | solution.py:86
  412.3 1.8 collective-permute-done.26
  414.7 2.5 constant_dynamic-slice_fusion
  417.2 1.5 copy.172
  419.6 2.5 copy.173
  422.2 2.4 copy.174
  424.6 2.5 copy.175
  428.9 1.5 copy.179
  430.4 2.3 bitcast_dynamic-update-slice_fusion.6
  432.7 2.2 bitcast_dynamic-update-slice_fusion.5
  439.8 4.3 multiply_reduce_fusion.2
  446.5 57.2 %psum.7 = f32[32,16]{0,1:T(8,128)S(1)} all-reduce(f32[32,16]{0,1:T(8,128)S(1)} %multiply_multiply_fusion.1), channel_id=1, replica_groups=mesh['dp'=8,'tensor'=4] {'dp','tensor'}, use_global_device_ids=true, to_apply=%region_4.5 | all-reduce | flops 512 | bytes 4096 | tf_op jit(solution)/shard_map/psum | solution.py:151
  504.5 1.7 multiply_reduce_fusion.3
  506.3 5.5 %multiply_reduce_fusion = f32[256]{0:T(256)S(1)} fusion(f32[7168]{0:T(1024)S(1)} %multiply_multiply_fusion, f32[256,7168]{1,0:T(8,128)} %bitcast_dynamic-update-slice_fusion, bf16[256,7168]{1,0:T(8,128)(2,1)} %param.10), kind=kLoop, calls=%fused_computation.1 | loop fusion | flops 7339776 | bytes 11039744 | tf_op jit(solution)/shard_map/reduce_sum | solution.py:165
  511.8 4.8 subtract_multiply_fusion
  (159 shorter events, 34.6 us)
Async XLA Ops:
  0.6 140.4 %collective-permute-start.9 = (bf16[1792,896]{1,0:T(8,128)(2,1)}, bf16[1792,896]{1,0:T(8,128)(2,1)}, u32[]{:S(2)}, u32[]{:S(2)}) collective-permute-start(bf16[1792,896]{1,0:T(8,128)(2,1)} %param.11), channel_id=1, source_target_pairs={{8,0},{12,4},{16,8},{20,12},{24,16},{28,20},{9,1},{13,5},{17,9},{2... | collective-permute-start | bytes 9633800 | tf_op jit(solution)/shard_map/ppermute | solution.py:73
  1.9 140.4 %collective-permute-start.6 = (bf16[1792,896]{1,0:T(8,128)(2,1)}, bf16[1792,896]{1,0:T(8,128)(2,1)}, u32[]{:S(2)}, u32[]{:S(2)}) collective-permute-start(bf16[1792,896]{1,0:T(8,128)(2,1)} %param.11), channel_id=1, source_target_pairs={{0,8},{4,12},{8,16},{12,20},{16,24},{20,28},{1,9},{5,13},{9,17},{1... | collective-permute-start | bytes 9633800 | tf_op jit(solution)/shard_map/ppermute | solution.py:73
  13.9 3.2 copy-start.21
  22.9 1.9 copy-start.7
  24.7 3.4 copy-start.23
  24.7 3.5 copy-start.24
  24.7 3.6 copy-start.20
  24.7 3.6 copy-start.17
  24.7 3.6 copy-start.19
  26.2 110.4 %collective-permute-start = (f32[512,896]{0,1:T(8,128)}, f32[512,896]{0,1:T(8,128)}, u32[]{:S(2)}, u32[]{:S(2)}) collective-permute-start(f32[512,896]{0,1:T(8,128)} %slice.181), channel_id=1, source_target_pairs={{0,1},{1,0},{2,3},{3,2},{4,5},{5,4},{6,7},{7,6},{8,9},{9,8},{10,11... | collective-permute-start | bytes 5505032 | tf_op jit(solution)/shard_map/ppermute | solution.py:86
  26.2 132.3 %collective-permute-start.2 = (bf16[1024,1792]{1,0:T(8,128)(2,1)}, bf16[1024,1792]{1,0:T(8,128)(2,1)}, u32[]{:S(2)}, u32[]{:S(2)}) collective-permute-start(bf16[1024,1792]{1,0:T(8,128)(2,1)} %bitcast.2), channel_id=1, source_target_pairs={{0,4},{4,0},{8,12},{12,8},{16,20},{20,16},{24,28},{28,24},{1,5},{5... | collective-permute-start | bytes 11010056 | tf_op jit(solution)/shard_map/ppermute | solution.py:77
  136.0 3.1 copy-start.3
  139.2 36.6 %collective-permute-start.1 = (f32[256,896]{0,1:T(8,128)S(1)}, f32[256,896]{0,1:T(8,128)S(1)}, u32[]{:S(2)}, u32[]{:S(2)}) collective-permute-start(f32[256,896]{0,1:T(8,128)S(1)} %slice.183), channel_id=1, source_target_pairs={{0,2},{1,3},{2,0},{3,1},{4,6},{5,7},{6,4},{7,5},{8,10},{9,11},{10,... | collective-permute-start | bytes 2752520 | tf_op jit(solution)/shard_map/ppermute | solution.py:86
  141.1 69.7 %collective-permute-start.10 = (bf16[1792,896]{1,0:T(8,128)(2,1)}, bf16[1792,896]{1,0:T(8,128)(2,1)}, u32[]{:S(2)}, u32[]{:S(2)}) collective-permute-start(bf16[1792,896]{1,0:T(8,128)(2,1)} %collective-permute-done.9), channel_id=1, source_target_pairs={{8,0},{12,4},{16,8},{20,12},{9,1},{13,5},{17,9},{21,13},{10,2},{14... | collective-permute-start | bytes 9633800 | tf_op jit(solution)/shard_map/ppermute | solution.py:73
  142.4 69.7 %collective-permute-start.7 = (bf16[1792,896]{1,0:T(8,128)(2,1)}, bf16[1792,896]{1,0:T(8,128)(2,1)}, u32[]{:S(2)}, u32[]{:S(2)}) collective-permute-start(bf16[1792,896]{1,0:T(8,128)(2,1)} %collective-permute-done.6), channel_id=1, source_target_pairs={{8,16},{12,20},{16,24},{20,28},{9,17},{13,21},{17,25},{21,29},{10,... | collective-permute-start | bytes 9633800 | tf_op jit(solution)/shard_map/ppermute | solution.py:73
  151.7 24.5 %collective-permute-start.14 = (f32[512,896]{0,1:T(8,128)S(1)}, f32[512,896]{0,1:T(8,128)S(1)}, u32[]{:S(2)}, u32[]{:S(2)}) collective-permute-start(f32[512,896]{0,1:T(8,128)S(1)} %slice.193), channel_id=1, source_target_pairs={{0,1},{1,0},{2,3},{3,2},{4,5},{5,4},{6,7},{7,6},{8,9},{9,8},{10,11... | collective-permute-start | bytes 5505032 | tf_op jit(solution)/shard_map/ppermute | solution.py:86
  158.3 1.9 copy-start.22
  158.5 62.8 %collective-permute-start.27 = (f32[512,896]{0,1:T(8,128)S(1)}, f32[512,896]{0,1:T(8,128)S(1)}, u32[]{:S(2)}, u32[]{:S(2)}) collective-permute-start(f32[512,896]{0,1:T(8,128)S(1)} %slice.213), channel_id=1, source_target_pairs={{0,1},{1,0},{2,3},{3,2},{4,5},{5,4},{6,7},{7,6},{8,9},{9,8},{10,11... | collective-permute-start | bytes 5505032 | tf_op jit(solution)/shard_map/ppermute | solution.py:86
  175.8 50.0 %collective-permute-start.3 = (f32[512,896]{0,1:T(8,128)}, f32[512,896]{0,1:T(8,128)}, u32[]{:S(2)}, u32[]{:S(2)}) collective-permute-start(f32[512,896]{0,1:T(8,128)} %slice.185), channel_id=1, source_target_pairs={{0,1},{1,0},{2,3},{3,2},{4,5},{5,4},{6,7},{7,6},{8,9},{9,8},{10,11... | collective-permute-start | bytes 5505032 | tf_op jit(solution)/shard_map/ppermute | solution.py:86
  176.3 52.7 %collective-permute-start.19 = (f32[512,896]{0,1:T(8,128)}, f32[512,896]{0,1:T(8,128)}, u32[]{:S(2)}, u32[]{:S(2)}) collective-permute-start(f32[512,896]{0,1:T(8,128)} %slice.201), channel_id=1, source_target_pairs={{0,1},{1,0},{2,3},{3,2},{4,5},{5,4},{6,7},{7,6},{8,9},{9,8},{10,11... | collective-permute-start | bytes 5505032 | tf_op jit(solution)/shard_map/ppermute | solution.py:86
  210.7 67.1 %collective-permute-start.11 = (bf16[1792,896]{1,0:T(8,128)(2,1)}, bf16[1792,896]{1,0:T(8,128)(2,1)}, u32[]{:S(2)}, u32[]{:S(2)}) collective-permute-start(bf16[1792,896]{1,0:T(8,128)(2,1)} %collective-permute-done.10), channel_id=1, source_target_pairs={{8,0},{12,4},{9,1},{13,5},{10,2},{14,6},{11,3},{15,7}} | collective-permute-start | bytes 9633800 | tf_op jit(solution)/shard_map/ppermute | solution.py:73
  212.0 65.8 %collective-permute-start.8 = (bf16[1792,896]{1,0:T(8,128)(2,1)}, bf16[1792,896]{1,0:T(8,128)(2,1)}, u32[]{:S(2)}, u32[]{:S(2)}) collective-permute-start(bf16[1792,896]{1,0:T(8,128)(2,1)} %collective-permute-done.7), channel_id=1, source_target_pairs={{16,24},{20,28},{17,25},{21,29},{18,26},{22,30},{19,27},{23,31}} | collective-permute-start | bytes 9633800 | tf_op jit(solution)/shard_map/ppermute | solution.py:73
  221.1 1.9 copy-start.12
  221.3 2.2 copy-start.15
  221.3 14.3 %collective-permute-start.29 = (f32[512,896]{0,1:T(8,128)S(1)}, f32[512,896]{0,1:T(8,128)S(1)}, u32[]{:S(2)}, u32[]{:S(2)}) collective-permute-start(f32[512,896]{0,1:T(8,128)S(1)} %slice.217), channel_id=1, source_target_pairs={{0,1},{1,0},{2,3},{3,2},{4,5},{5,4},{6,7},{7,6},{8,9},{9,8},{10,11... | collective-permute-start | bytes 5505032 | tf_op jit(solution)/shard_map/ppermute | solution.py:86
  223.7 1.5 copy-start.16
  228.7 6.9 %copy-start.13 = (f32[1024,896]{0,1:T(8,128)S(1)}, f32[1024,896]{0,1:T(8,128)}, u32[]{:S(2)}) copy-start(f32[1024,896]{0,1:T(8,128)} %copy-done.12) | copy-start | bytes 11010052
  228.7 74.6 %collective-permute-start.4 = (f32[256,896]{0,1:T(8,128)}, f32[256,896]{0,1:T(8,128)}, u32[]{:S(2)}, u32[]{:S(2)}) collective-permute-start(f32[256,896]{0,1:T(8,128)} %slice.187), channel_id=1, source_target_pairs={{0,2},{1,3},{2,0},{3,1},{4,6},{5,7},{6,4},{7,5},{8,10},{9,11},{10,... | collective-permute-start | bytes 2752520 | tf_op jit(solution)/shard_map/ppermute | solution.py:86
  232.1 72.9 %collective-permute-start.20 = (f32[256,896]{0,1:T(8,128)}, f32[256,896]{0,1:T(8,128)}, u32[]{:S(2)}, u32[]{:S(2)}) collective-permute-start(f32[256,896]{0,1:T(8,128)} %slice.203), channel_id=1, source_target_pairs={{0,2},{1,3},{2,0},{3,1},{4,6},{5,7},{6,4},{7,5},{8,10},{9,11},{10,... | collective-permute-start | bytes 2752520 | tf_op jit(solution)/shard_map/ppermute | solution.py:86
  237.1 70.1 %collective-permute-start.30 = (f32[256,896]{0,1:T(8,128)}, f32[256,896]{0,1:T(8,128)}, u32[]{:S(2)}, u32[]{:S(2)}) collective-permute-start(f32[256,896]{0,1:T(8,128)} %slice.219), channel_id=1, source_target_pairs={{8,10},{9,11},{10,8},{11,9},{12,14},{13,15},{14,12},{15,13},{16,18... | collective-permute-start | bytes 2752520 | tf_op jit(solution)/shard_map/ppermute | solution.py:86
  284.4 2.5 copy-start.10
  286.9 22.0 %collective-permute-start.16 = (f32[512,896]{0,1:T(8,128)}, f32[512,896]{0,1:T(8,128)}, u32[]{:S(2)}, u32[]{:S(2)}) collective-permute-start(f32[512,896]{0,1:T(8,128)} %slice.197), channel_id=1, source_target_pairs={{0,1},{1,0},{2,3},{3,2},{4,5},{5,4},{6,7},{7,6},{8,9},{9,8},{10,11... | collective-permute-start | bytes 5505032 | tf_op jit(solution)/shard_map/ppermute | solution.py:86
  293.5 2.4 copy-start.8
  295.8 34.5 %collective-permute-start.24 = (f32[512,896]{0,1:T(8,128)}, f32[512,896]{0,1:T(8,128)}, u32[]{:S(2)}, u32[]{:S(2)}) collective-permute-start(f32[512,896]{0,1:T(8,128)} %slice.209), channel_id=1, source_target_pairs={{0,1},{1,0},{2,3},{3,2},{4,5},{5,4},{6,7},{7,6},{8,9},{9,8},{10,11... | collective-permute-start | bytes 5505032 | tf_op jit(solution)/shard_map/ppermute | solution.py:86
  303.3 8.2 %copy-start.11 = (f32[1024,896]{0,1:T(8,128)S(1)}, f32[1024,896]{0,1:T(8,128)}, u32[]{:S(2)}) copy-start(f32[1024,896]{0,1:T(8,128)} %copy-done.10) | copy-start | bytes 11010052
  303.3 31.7 %collective-permute-start.12 = (f32[512,896]{0,1:T(8,128)S(1)}, f32[512,896]{0,1:T(8,128)S(1)}, u32[]{:S(2)}, u32[]{:S(2)}) collective-permute-start(f32[512,896]{0,1:T(8,128)S(1)} %slice.189), channel_id=1, source_target_pairs={{0,1},{1,0},{2,3},{3,2},{4,5},{5,4},{6,7},{7,6},{8,9},{9,8},{10,11... | collective-permute-start | bytes 5505032 | tf_op jit(solution)/shard_map/ppermute | solution.py:86
  304.9 22.9 %collective-permute-start.5 = (f32[256,896]{0,1:T(8,128)S(1)}, f32[256,896]{0,1:T(8,128)S(1)}, u32[]{:S(2)}, u32[]{:S(2)}) collective-permute-start(f32[256,896]{0,1:T(8,128)S(1)} %slice_add_fusion.18), channel_id=1, source_target_pairs={{0,4},{4,0},{8,12},{12,8},{16,20},{20,16},{24,28},{28,24},{1,5},{5... | collective-permute-start | bytes 2752520 | tf_op jit(solution)/shard_map/ppermute | solution.py:77
  307.1 49.3 %collective-permute-start.22 = (f32[512,896]{0,1:T(8,128)S(1)}, f32[512,896]{0,1:T(8,128)S(1)}, u32[]{:S(2)}, u32[]{:S(2)}) collective-permute-start(f32[512,896]{0,1:T(8,128)S(1)} %slice.205), channel_id=1, source_target_pairs={{0,1},{1,0},{2,3},{3,2},{4,5},{5,4},{6,7},{7,6},{8,9},{9,8},{10,11... | collective-permute-start | bytes 5505032 | tf_op jit(solution)/shard_map/ppermute | solution.py:86
  308.9 24.1 %copy-start.9 = (f32[1024,896]{0,1:T(8,128)S(1)}, f32[1024,896]{0,1:T(8,128)}, u32[]{:S(2)}) copy-start(f32[1024,896]{0,1:T(8,128)} %copy-done.8) | copy-start | bytes 11010052
  308.9 65.3 %collective-permute-start.15 = (f32[256,896]{0,1:T(8,128)S(1)}, f32[256,896]{0,1:T(8,128)S(1)}, u32[]{:S(2)}, u32[]{:S(2)}) collective-permute-start(f32[256,896]{0,1:T(8,128)S(1)} %slice.195), channel_id=1, source_target_pairs={{0,2},{1,3},{2,0},{3,1},{4,6},{5,7},{6,4},{7,5},{8,10},{9,11},{10,... | collective-permute-start | bytes 2752520 | tf_op jit(solution)/shard_map/ppermute | solution.py:86
  327.9 26.0 %collective-permute-start.17 = (f32[256,896]{0,1:T(8,128)S(1)}, f32[256,896]{0,1:T(8,128)S(1)}, u32[]{:S(2)}, u32[]{:S(2)}) collective-permute-start(f32[256,896]{0,1:T(8,128)S(1)} %slice.199), channel_id=1, source_target_pairs={{0,2},{1,3},{2,0},{3,1},{4,6},{5,7},{6,4},{7,5},{24,26},{25,27},{2... | collective-permute-start | bytes 2752520 | tf_op jit(solution)/shard_map/ppermute | solution.py:86
  330.4 64.6 %collective-permute-start.21 = (f32[256,896]{0,1:T(8,128)S(1)}, f32[256,896]{0,1:T(8,128)S(1)}, u32[]{:S(2)}, u32[]{:S(2)}) collective-permute-start(f32[256,896]{0,1:T(8,128)S(1)} %slice_add_fusion.14), channel_id=1, source_target_pairs={{0,4},{4,0},{8,12},{12,8},{16,20},{20,16},{1,5},{5,1},{9,13},{13,9... | collective-permute-start | bytes 2752520 | tf_op jit(solution)/shard_map/ppermute | solution.py:77
  335.0 38.6 %collective-permute-start.25 = (f32[256,896]{0,1:T(8,128)S(1)}, f32[256,896]{0,1:T(8,128)S(1)}, u32[]{:S(2)}, u32[]{:S(2)}) collective-permute-start(f32[256,896]{0,1:T(8,128)S(1)} %slice.211), channel_id=1, source_target_pairs={{0,2},{1,3},{2,0},{3,1},{4,6},{5,7},{6,4},{7,5},{8,10},{9,11},{10,... | collective-permute-start | bytes 2752520 | tf_op jit(solution)/shard_map/ppermute | solution.py:86
  353.9 39.3 %collective-permute-start.13 = (f32[256,896]{0,1:T(8,128)S(1)}, f32[256,896]{0,1:T(8,128)S(1)}, u32[]{:S(2)}, u32[]{:S(2)}) collective-permute-start(f32[256,896]{0,1:T(8,128)S(1)} %slice.191), channel_id=1, source_target_pairs={{0,2},{1,3},{2,0},{3,1},{4,6},{5,7},{6,4},{7,5},{24,26},{25,27},{2... | collective-permute-start | bytes 2752520 | tf_op jit(solution)/shard_map/ppermute | solution.py:86
  356.4 39.5 %collective-permute-start.18 = (f32[256,896]{0,1:T(8,128)S(1)}, f32[256,896]{0,1:T(8,128)S(1)}, u32[]{:S(2)}, u32[]{:S(2)}) collective-permute-start(f32[256,896]{0,1:T(8,128)S(1)} %slice_add_fusion.15), channel_id=1, source_target_pairs={{0,4},{4,0},{24,28},{28,24},{1,5},{5,1},{25,29},{29,25},{2,6},{6,2... | collective-permute-start | bytes 2752520 | tf_op jit(solution)/shard_map/ppermute | solution.py:77
  373.6 38.5 %collective-permute-start.23 = (f32[256,896]{0,1:T(8,128)S(1)}, f32[256,896]{0,1:T(8,128)S(1)}, u32[]{:S(2)}, u32[]{:S(2)}) collective-permute-start(f32[256,896]{0,1:T(8,128)S(1)} %slice.207), channel_id=1, source_target_pairs={{0,2},{1,3},{2,0},{3,1},{4,6},{5,7},{6,4},{7,5},{8,10},{9,11},{10,... | collective-permute-start | bytes 2752520 | tf_op jit(solution)/shard_map/ppermute | solution.py:86
  374.2 39.9 %collective-permute-start.28 = (f32[256,896]{0,1:T(8,128)S(1)}, f32[256,896]{0,1:T(8,128)S(1)}, u32[]{:S(2)}, u32[]{:S(2)}) collective-permute-start(f32[256,896]{0,1:T(8,128)S(1)} %slice.215), channel_id=1, source_target_pairs={{8,10},{9,11},{10,8},{11,9},{12,14},{13,15},{14,12},{15,13},{16,18... | collective-permute-start | bytes 2752520 | tf_op jit(solution)/shard_map/ppermute | solution.py:86
  393.2 20.8 %collective-permute-start.26 = (f32[256,896]{0,1:T(8,128)S(1)}, f32[256,896]{0,1:T(8,128)S(1)}, u32[]{:S(2)}, u32[]{:S(2)}) collective-permute-start(f32[256,896]{0,1:T(8,128)S(1)} %slice_add_fusion.12), channel_id=1, source_target_pairs={{0,4},{4,0},{8,12},{12,8},{16,20},{20,16},{24,28},{28,24},{1,5},{5... | collective-permute-start | bytes 2752520 | tf_op jit(solution)/shard_map/ppermute | solution.py:77
  395.0 19.6 %collective-permute-start.31 = (f32[256,896]{0,1:T(8,128)S(1)}, f32[256,896]{0,1:T(8,128)S(1)}, u32[]{:S(2)}, u32[]{:S(2)}) collective-permute-start(f32[256,896]{0,1:T(8,128)S(1)} %slice_add_fusion.10), channel_id=1, source_target_pairs={{8,12},{12,8},{16,20},{20,16},{24,28},{28,24},{9,13},{13,9},{17,21... | collective-permute-start | bytes 2752520 | tf_op jit(solution)/shard_map/ppermute | solution.py:77
  419.6 7.4 %copy-start.14 = (f32[1,256,896]{1,2,0:T(8,128)S(1)}, f32[1,256,896]{1,2,0:T(8,128)}, u32[]{:S(2)}) copy-start(f32[1,256,896]{1,2,0:T(8,128)} %get-tuple-element.14) | copy-start | bytes 2752516
  430.4 4.5 copy-start.6
  430.4 5.5 %copy-start.5 = (f32[1,256,896]{2,1,0:T(8,128)S(1)}, f32[1,256,896]{2,1,0:T(8,128)}, u32[]{:S(2)}) copy-start(f32[1,256,896]{2,1,0:T(8,128)} %copy.176) | copy-start | bytes 2752516
  435.9 3.9 copy-start.1
  439.8 5.2 copy-start
  445.0 1.2 copy-start.18
  445.0 1.2 copy-start.4
  445.0 66.8 %slice-start = ((s8[7340032]{0:T(1024)(128)(4,1)}), s8[3145728]{0:T(1024)(128)(4,1)S(1)}, s32[]{:S(2)}) async-start(s8[7340032]{0:T(1024)(128)(4,1)} %bitcast.65), calls=%async_computation | async-start | bytes 6291456
  503.8 8.0 %slice-start.1 = ((s8[7340032]{0:T(1024)(128)(4,1)}), s8[4194304]{0:T(1024)(128)(4,1)S(1)}, s32[]{:S(2)}) async-start(s8[7340032]{0:T(1024)(128)(4,1)} %bitcast.65), calls=%async_computation.1 | async-start | bytes 8388608
  506.3 5.5 %copy-start.2 = (bf16[256,7168]{1,0:T(8,128)(2,1)S(1)}, bf16[256,7168]{1,0:T(8,128)(2,1)}, u32[]{:S(2)}) copy-start(bf16[256,7168]{1,0:T(8,128)(2,1)} %param.10) | copy-start | bytes 11010052
